TPU v7x, 32 devices: a whole 2x2x4 slice. The times are simulated.
32 devices in a mesh: ep: 16 (over z, x, core), tp: 2 (over y).
Axes of the slice: x: 2, y: 2, z: 4, core: 2. Of those that a mesh axis runs over, the one named last changes fastest.
Arguments:
- attn: bfloat16 [2048, 2048], P('ep', 'tp'), may hold values from -6 to 6
- o_weight: bfloat16 [2048, 2048], P('tp'), may hold values from -0.125 to 0.125
- residual: bfloat16 [2048, 2048], P(('ep', 'tp')), may hold values from -6 to 6
- norm_gain: float32 [2048], replicated, may hold values from 0.5 to 2
- routes: int32 [2048, 6], P('ep'), may hold values from 0 to 15, all different within a row; in each aligned block of 64 rows (0 to 63, 64 to 127, ...) at most 32 rows name the same one
- route_logits: float32 [2048, 6], P('ep'), may hold values from -6 to 6
- expert_in: bfloat16 [16, 2, 2048, 1408], P('ep', None, None, 'tp'), may hold values from -0.125 to 0.125
- expert_out: bfloat16 [16, 2048, 1408], P('ep', None, 'tp'), may hold values from -0.15625 to 0.15625
- shared_in: bfloat16 [2, 2048, 1408], P(None, None, 'tp'), may hold values from -0.125 to 0.125
- shared_out: bfloat16 [2048, 1408], P(None, 'tp'), may hold values from -0.15625 to 0.15625
Outputs:
- block_out: bfloat16 [2048, 2048], P(('ep', 'tp'))
Inputs may be any that keep to these rules, and one draw needn't show every extreme that they name: `routes`: each row names 6 different experts. Within each aligned block of 64 rows (the rows of one device) no expert is named by more than 32 rows, a bound that some block reaches.
All inputs are finite; a program needn't handle non-finite values.
Results may differ from a plain program's by a relative error of at most 0.0058.
Values may be sent and summed in bfloat16 or wider, within the bound.
A program may use at most 192 MiB of HBM per device.

v0:
```python
import jax
import jax.numpy as jnp
from jax import lax
from jax.sharding import PartitionSpec as P


def slot_places(route_rows, capacity, experts):
    flat_routes = route_rows.reshape(-1)
    onehot = (flat_routes[:, None] == jnp.arange(experts, dtype=jnp.int32)[None, :]).astype(
        jnp.int32
    )
    before = jnp.cumsum(onehot, axis=0) - onehot
    ranks = jnp.sum(before * onehot, axis=1)
    return flat_routes * capacity + ranks


def fill_slots(source_rows, places, capacity, experts, topk):
    copies = jnp.repeat(source_rows, topk, axis=0)
    empty_slots = jnp.zeros((experts * capacity, source_rows.shape[1]), source_rows.dtype)
    return empty_slots.at[places].set(copies)


def route_weights(logits):
    sigmoids = jax.nn.sigmoid(logits)
    return 2.446 * sigmoids / jnp.sum(sigmoids, axis=-1, keepdims=True)


def expert_part(slots, w_in, w_out):
    gate_val = jnp.einsum("slcd,ldf->slcf", slots, w_in[:, 0], preferred_element_type=jnp.float32)
    up_val = jnp.einsum("slcd,ldf->slcf", slots, w_in[:, 1], preferred_element_type=jnp.float32)
    active = (jax.nn.silu(gate_val) * up_val).astype(jnp.bfloat16)
    return jnp.einsum("slcf,ldf->slcd", active, w_out, preferred_element_type=jnp.float32)


def shared_part(source_rows, s_in, s_out):
    gate_val = jnp.dot(source_rows, s_in[0], preferred_element_type=jnp.float32)
    up_val = jnp.dot(source_rows, s_in[1], preferred_element_type=jnp.float32)
    active = (jax.nn.silu(gate_val) * up_val).astype(jnp.bfloat16)
    return jnp.einsum("tf,df->td", active, s_out, preferred_element_type=jnp.float32)


def combine_slots(values, places, weights, topk):
    picked = values[places].reshape(-1, topk, values.shape[1])
    return jnp.sum(picked * weights[:, :, None], axis=1)


def slotted_shards(
    attn,
    o_weight,
    residual,
    norm_gain,
    routes,
    route_logits,
    expert_in,
    expert_out,
    shared_in,
    shared_out,
):
    tok_rows = residual.shape[0]
    width = residual.shape[1]
    topk = routes.shape[1]
    tp_count = lax.axis_size("tp")
    ep_count = lax.axis_size("ep")
    local_experts = expert_in.shape[0]
    experts = local_experts * ep_count
    capacity = max(2, (4 * tok_rows * topk + 3 * experts - 1) // (3 * experts))
    attn_out = lax.psum_scatter(
        jnp.dot(attn, o_weight, preferred_element_type=jnp.float32),
        "tp",
        scatter_dimension=0,
        tiled=True,
    )
    hidden = residual.astype(jnp.float32) + attn_out
    inv_norm = lax.rsqrt(jnp.mean(hidden * hidden, axis=-1, keepdims=True) + 1e-06)
    normed = (hidden * inv_norm * norm_gain).astype(jnp.bfloat16)
    group_rows = lax.all_gather(normed, "tp", axis=0, tiled=True)
    group_cap = tp_count * capacity
    places = slot_places(routes, group_cap, experts)
    outgoing = fill_slots(group_rows, places, group_cap, experts, topk)
    incoming = lax.all_to_all(outgoing, "ep", split_axis=0, concat_axis=0, tiled=True)
    partial_value = expert_part(
        incoming.reshape(ep_count, local_experts, group_cap, width), expert_in, expert_out
    )
    returned = lax.all_to_all(
        partial_value.reshape(-1, width), "ep", split_axis=0, concat_axis=0, tiled=True
    )
    mixture = combine_slots(returned, places, route_weights(route_logits), topk)
    mixture = mixture + shared_part(group_rows, shared_in, shared_out)
    moe_sum = lax.psum_scatter(mixture, "tp", scatter_dimension=0, tiled=True)
    return (hidden + moe_sum).astype(jnp.bfloat16)


def tp_sum_scatter(rows):
    count = lax.axis_size("tp")
    if count != 2:
        return lax.psum_scatter(rows, "tp", scatter_dimension=0, tiled=True)
    me = lax.axis_index("tp")
    each = rows.shape[0] // count
    away = lax.dynamic_slice_in_dim(rows, (1 - me) * each, each, 0).astype(jnp.bfloat16)
    arrived = lax.ppermute(away, "tp", [(0, 1), (1, 0)])
    own = lax.dynamic_slice_in_dim(rows, me * each, each, 0)
    return own + arrived.astype(jnp.float32)


def dense_shards(
    attn,
    o_weight,
    residual,
    norm_gain,
    routes,
    route_logits,
    expert_in,
    expert_out,
    shared_in,
    shared_out,
):
    local_experts = expert_in.shape[0]
    ep_count = lax.axis_size("ep")
    experts = local_experts * ep_count
    ep_me = lax.axis_index("ep")
    weights = route_weights(route_logits)
    chosen = routes[:, :, None] == jnp.arange(experts, dtype=jnp.int32)[None, None, :]
    dense_weights = jnp.sum(jnp.where(chosen, weights[:, :, None], 0.0), axis=1)
    all_weights = lax.all_gather(dense_weights, "ep", axis=0, tiled=True)
    my_weights = lax.dynamic_slice_in_dim(all_weights, ep_me * local_experts, local_experts, 1)

    attn_out = tp_sum_scatter(jnp.dot(attn, o_weight, preferred_element_type=jnp.float32))
    hidden = residual.astype(jnp.float32) + attn_out
    inv_norm = lax.rsqrt(jnp.mean(hidden * hidden, axis=-1, keepdims=True) + 1e-06)
    normed = (hidden * inv_norm * norm_gain).astype(jnp.bfloat16)
    all_rows = lax.all_gather(normed, ("ep", "tp"), axis=0, tiled=True)
    group_rows = lax.all_gather(normed, "tp", axis=0, tiled=True) if lax.axis_size("tp") != 2 else None
    if group_rows is None:
        other = lax.ppermute(normed, "tp", [(0, 1), (1, 0)])
        first = lax.axis_index("tp") == 0
        group_rows = jnp.concatenate(
            [jnp.where(first, normed, other), jnp.where(first, other, normed)], axis=0
        )
    shared = tp_sum_scatter(shared_part(group_rows, shared_in, shared_out))
    partial = None
    for item in range(local_experts):
        gate_val = jnp.dot(all_rows, expert_in[item, 0], preferred_element_type=jnp.float32)
        up_val = jnp.dot(all_rows, expert_in[item, 1], preferred_element_type=jnp.float32)
        active = (jax.nn.silu(gate_val) * up_val).astype(jnp.bfloat16)
        value = jnp.einsum("tf,df->td", active, expert_out[item], preferred_element_type=jnp.float32)
        value = value * my_weights[:, item : item + 1]
        partial = value if partial is None else partial + value
    mixture = lax.psum_scatter(
        partial.astype(jnp.bfloat16), ("ep", "tp"), scatter_dimension=0, tiled=True
    )
    return (hidden + shared + mixture.astype(jnp.float32)).astype(jnp.bfloat16)


def shards(*args):
    routes, expert_in = args[4], args[6]
    experts = expert_in.shape[0] * lax.axis_size("ep")
    if experts <= 4 * routes.shape[1]:
        return dense_shards(*args)
    return slotted_shards(*args)


def solution(mesh):
    in_specs = (
        P("ep", "tp"),
        P("tp", None),
        P(("ep", "tp"), None),
        P(),
        P("ep", None),
        P("ep", None),
        P("ep", None, None, "tp"),
        P("ep", None, "tp"),
        P(None, None, "tp"),
        P(None, "tp"),
    )
    out_specs = P(("ep", "tp"), None)
    return jax.shard_map(shards, mesh=mesh, in_specs=in_specs, out_specs=out_specs, check_vma=False)
```

profile of v0, /device:TPU:0, one launch (start us, length us, event | category | flops | bytes accessed | tf_op | source)
XLA Modules:
  0.0 331.4 jit_solution(5927637871507394894)
XLA Ops:
  6.5 0.0 all-gather.2.cloned.1.call-start
  6.6 4.1 %fusion.27 = f32[128,2048]{1,0:T(8,128)} fusion(bf16[128,1024]{1,0:T(8,128)(2,1)} %param.10, bf16[1024,2048]{1,0:T(8,128)(2,1)} %param.11), kind=kOutput, calls=%fused_computation.38 | convolution fusion | flops 536870912 | bytes 5505024 | tf_op jit(solution)/shard_map/dot_general | solution.py:127
  10.7 1.1 dynamic-slice_convert_fusion.1
  11.8 3.1 collective-permute-start
  14.8 6.4 %collective-permute-done = bf16[64,2048]{1,0:T(8,128)(2,1)} collective-permute-done((bf16[64,2048]{1,0:T(8,128)(2,1)S(1)}, bf16[64,2048]{1,0:T(8,128)(2,1)}, u32[]{:S(2)}, u32[]{:S(2)}) %collective-permute-start) | collective-permute-done | bytes 262176 | tf_op jit(solution)/shard_map/ppermute | solution.py:100
  21.2 1.4 multiply_reduce_fusion
  22.7 0.8 multiply_convert_fusion.2
  23.5 0.0 reduce-scatter.2.cloned.1.call-start
  23.6 22.4 %all_gather.7 = f32[2048,16]{0,1:T(8,128)S(1)} all-gather(f32[128,16]{0,1:T(8,128)S(1)} %select_reduce_fusion), channel_id=1, replica_groups=mesh['ep'=16,'tp'=2] {'ep'}, dimensions={0}, use_global_device_ids=true | all-gather | bytes 139264 | tf_op jit(solution)/shard_map/all_gather | solution.py:124
  46.0 56.1 %all-gather.2.cloned.1.call-done = bf16[2048,2048]{1,0:T(8,128)(2,1)} async-done(((bf16[64,2048]{1,0:T(8,128)(2,1)}), bf16[2048,2048]{1,0:T(8,128)(2,1)}) %all-gather.2.cloned.1.call-update) | async-done | bytes 8388624 | tf_op jit(solution)/shard_map/all_gather | solution.py:131
  102.1 11.8 %fusion.3 = f32[2048,704]{0,1:T(8,128)} fusion(bf16[2048,2048]{1,0:T(8,128)(2,1)} %all-gather.2.cloned.1.call-done, bf16[1,2,2048,704]{2,3,1,0:T(8,128)(2,1)} %param.16), kind=kOutput, calls=%fused_computation.4 | convolution fusion | flops 5905580032 | bytes 17039360 | tf_op jit(solution)/shard_map/dot_general | solution.py:142
  114.0 19.1 %multiply_convert_fusion = bf16[2048,2048]{1,0:T(8,128)(2,1)} fusion(f32[2048]{0:T(1024)S(1)} %bitcast.26, f32[2048,704]{0,1:T(8,128)} %fusion.3, bf16[2048,2048]{1,0:T(8,128)(2,1)} %all-gather.2.cloned.1.call-done, bf16[1,2048,704]{1,2,0:T(8,128)(2,1)S(1)} %copy-done, bf16[1,2,2048,704]{2,3,1,0:T(8,128)(2,1)} %param.16), kind=kOutput, calls=%fused_computation | convolution fusion | flops 11828199424 | bytes 28319744 | tf_op jit(solution)/shard_map/tf,df->td/dot_general | solution.py:145
  133.1 1.5 collective-permute-start.1
  134.6 11.4 %collective-permute-done.1 = bf16[64,2048]{1,0:T(8,128)(2,1)} collective-permute-done((bf16[64,2048]{1,0:T(8,128)(2,1)}, bf16[64,2048]{1,0:T(8,128)(2,1)}, u32[]{:S(2)}, u32[]{:S(2)}) %collective-permute-start.1) | collective-permute-done | bytes 262176 | tf_op jit(solution)/shard_map/ppermute | solution.py:134
  146.0 1.1 broadcast_select_fusion.1
  147.2 0.7 copy-done.1
  147.9 0.1 copy-done.2
  148.0 3.5 %fusion.7 = f32[128,704]{0,1:T(8,128)} fusion(bf16[2,2048,704]{1,2,0:T(8,128)(2,1)} %param.18, bf16[64,2048]{1,0:T(8,128)(2,1)S(1)} %get-tuple-element.8, bf16[64,2048]{1,0:T(8,128)(2,1)S(1)} %get-tuple-element.7), kind=kOutput, calls=%fused_computation.8 | convolution fusion | flops 370147328 | bytes 3768320 | tf_op jit(solution)/shard_map/dot_general | solution.py:36
  151.4 6.2 %fusion.18 = f32[128,2048]{1,0:T(8,128)} fusion(bf16[2048,704]{0,1:T(8,128)(2,1)} %param.19, f32[128,704]{0,1:T(8,128)} %fusion.7, bf16[2,2048,704]{1,2,0:T(8,128)(2,1)} %param.18, bf16[64,2048]{1,0:T(8,128)(2,1)} %copy-done.2, bf16[64,2048]{1,0:T(8,128)(2,1)} %copy-done.1), kind=kOutput, calls=%fused_computation.23 | convolution fusion | flops 739786752 | bytes 7700480 | tf_op jit(solution)/shard_map/tf,df->td/dot_general | solution.py:39
  157.6 1.1 dynamic-slice_convert_fusion
  158.7 2.4 collective-permute-start.2
  161.1 12.4 %collective-permute-done.2 = bf16[64,2048]{1,0:T(8,128)(2,1)} collective-permute-done((bf16[64,2048]{1,0:T(8,128)(2,1)S(1)}, bf16[64,2048]{1,0:T(8,128)(2,1)}, u32[]{:S(2)}, u32[]{:S(2)}) %collective-permute-start.2) | collective-permute-done | bytes 262176 | tf_op jit(solution)/shard_map/ppermute | solution.py:100
  173.5 149.1 %reduce-scatter.2.cloned.1.call-done = bf16[64,2048]{1,0:T(8,128)(2,1)} async-done(((bf16[2048,2048]{1,0:T(8,128)(2,1)}), bf16[64,2048]{1,0:T(8,128)(2,1)}) %reduce-scatter.2.cloned.1.call-update) | async-done | bytes 262160 | tf_op jit(solution)/shard_map/reduce_scatter | solution.py:148
  322.6 2.0 add_convert_fusion
  (17 shorter events, 0.1 us)
Async XLA Ops:
  6.5 107.4 %copy-start = (bf16[1,2048,704]{1,2,0:T(8,128)(2,1)S(1)}, bf16[1,2048,704]{1,2,0:T(8,128)(2,1)}, u32[]{:S(2)}) copy-start(bf16[1,2048,704]{1,2,0:T(8,128)(2,1)} %param.17) | copy-start | bytes 8650756
  6.5 16.1 %copy-start.3 = (f32[2048]{0:T(1024)S(1)}, f32[2048]{0:T(1024)}, u32[]{:S(2)}) copy-start(f32[2048]{0:T(1024)} %param.13) | copy-start | bytes 24580
  6.5 17.0 %copy-start.4 = (f32[128,6]{0,1:T(8,128)S(1)}, f32[128,6]{0,1:T(8,128)}, u32[]{:S(2)}) copy-start(f32[128,6]{0,1:T(8,128)} %param.15) | copy-start | bytes 9220
  6.5 17.1 %copy-start.5 = (s32[128,6]{0,1:T(8,128)S(1)}, s32[128,6]{0,1:T(8,128)}, u32[]{:S(2)}) copy-start(s32[128,6]{0,1:T(8,128)} %param.14) | copy-start | bytes 9220
  6.5 95.6 %all-gather.2.cloned.1.call-start = ((), (), s32[]{:S(2)}) async-start(), calls=%async_computation.1 | async-start | bytes 8650752 | tf_op jit(solution)/shard_map/all_gather | solution.py:131
  11.8 9.5 %collective-permute-start = (bf16[64,2048]{1,0:T(8,128)(2,1)S(1)}, bf16[64,2048]{1,0:T(8,128)(2,1)}, u32[]{:S(2)}, u32[]{:S(2)}) collective-permute-start(bf16[64,2048]{1,0:T(8,128)(2,1)S(1)} %dynamic-slice_convert_fusion.1), channel_id=1, source_target_pairs={{0,1},{1,0},{2,3},{3,2},{4,5},{5,4},{6,7},{7,6},{8,9},{9,8},{10,11... | collective-permute-start | bytes 786440 | tf_op jit(solution)/shard_map/ppermute | solution.py:100
  23.5 299.1 %reduce-scatter.2.cloned.1.call-start = ((), (), s32[]{:S(2)}) async-start(), calls=%async_computation.2 | async-start | bytes 8650752 | tf_op jit(solution)/shard_map/reduce_scatter | solution.py:148
  133.1 12.9 %collective-permute-start.1 = (bf16[64,2048]{1,0:T(8,128)(2,1)}, bf16[64,2048]{1,0:T(8,128)(2,1)}, u32[]{:S(2)}, u32[]{:S(2)}) collective-permute-start(bf16[64,2048]{1,0:T(8,128)(2,1)} %multiply_convert_fusion.2), channel_id=1, source_target_pairs={{0,1},{1,0},{2,3},{3,2},{4,5},{5,4},{6,7},{7,6},{8,9},{9,8},{10,11... | collective-permute-start | bytes 786440 | tf_op jit(solution)/shard_map/ppermute | solution.py:134
  147.2 0.7 copy-start.1
  147.2 0.8 copy-start.2
  158.7 14.8 %collective-permute-start.2 = (bf16[64,2048]{1,0:T(8,128)(2,1)S(1)}, bf16[64,2048]{1,0:T(8,128)(2,1)}, u32[]{:S(2)}, u32[]{:S(2)}) collective-permute-start(bf16[64,2048]{1,0:T(8,128)(2,1)S(1)} %dynamic-slice_convert_fusion), channel_id=1, source_target_pairs={{0,1},{1,0},{2,3},{3,2},{4,5},{5,4},{6,7},{7,6},{8,9},{9,8},{10,11... | collective-permute-start | bytes 786440 | tf_op jit(solution)/shard_map/ppermute | solution.py:100
Sparse Core Ops, SparseCore 0:
  23.6 78.4 all-gather.1
  133.2 189.3 reduce-scatter.1
where the time goes:
time: 332 us; the launch traced here: 331 us
  waiting for transfers between devices  235 us (71%)
  matrix products  44.7 us (13%)
  blocking collectives  22.4 us (7%)
  between operations  13.5 us (4%)
  starting transfers between devices  7.06 us (2%)
  other arithmetic  5.41 us (2%)
    reduce_scatter x1, waiting for transfers between devices, dense_shards(): lax.psum_scatter(partial.astype(jnp.bfloat16), ('ep', 'tp'), scatter_dime...  149 us
    all_gather x1, waiting for transfers between devices, dense_shards(): all_rows = lax.all_gather(normed, ('ep', 'tp'), axis=0, tiled=True)  56.1 us
    all_gather x1, blocking collectives, dense_shards(): all_weights = lax.all_gather(dense_weights, 'ep', axis=0, tiled=True)  22.4 us
    dot_general x1, matrix products, dense_shards(): jnp.einsum('tf,df->td', active, expert_out[item], preferred_element_type=...  19.1 us
    ppermute x2, waiting for transfers between devices, tp_sum_scatter(): arrived = lax.ppermute(away, 'tp', [(0, 1), (1, 0)])  18.8 us
    dot_general x1, matrix products, dense_shards(): jnp.dot(all_rows, expert_in[item, 0], preferred_element_type=jnp.float32)  11.8 us
    ppermute x1, waiting for transfers between devices, dense_shards(): other = lax.ppermute(normed, 'tp', [(0, 1), (1, 0)])  11.4 us
  transfers between devices with their start and end apart: 5, of which 5 were waited for; matrix products, arithmetic and copies ran while one was open for 4% of the time, Pallas kernels for 0%

commit v1 on v0

--- a/solution.py
+++ b/solution.py
@@ -1,7 +1,11 @@
 import jax
 import jax.numpy as jnp
 from jax import lax
+from jax.experimental import pallas as pl
+from jax.experimental.pallas import tpu as pltpu
 from jax.sharding import PartitionSpec as P
+
+PIECES = 4
 
 
 def slot_places(route_rows, capacity, experts):
@@ -90,6 +94,229 @@
     return (hidden + moe_sum).astype(jnp.bfloat16)
 
 
+def place():
+    ep = lax.axis_index("ep")
+    return lax.div(ep, 4), lax.rem(lax.div(ep, 2), 2), lax.rem(ep, 2), lax.axis_index("tp")
+
+
+def device_at(z, x, core, y):
+    return (z * 4 + x * 2 + core, y)
+
+
+def peers(z, x, core, y):
+    along_z = [device_at(lax.rem(z + step, 4), x, core, y) for step in (1, 2, 3)]
+    return (
+        along_z,
+        device_at(z, 1 - x, core, y),
+        device_at(z, x, 1 - core, y),
+        device_at(z, x, core, 1 - y),
+    )
+
+
+def greet(along_z, x_peer, core_peer, y_peer):
+    barrier = pltpu.get_barrier_semaphore()
+    for peer in (*along_z, x_peer, core_peer, y_peer):
+        pl.semaphore_signal(
+            barrier, inc=1, device_id=peer, device_id_type=pl.DeviceIdType.MESH
+        )
+    pl.semaphore_wait(barrier, 6)
+
+
+def remote(src, dst, send_sem, recv_sem, peer):
+    copy = pltpu.make_async_remote_copy(
+        src_ref=src,
+        dst_ref=dst,
+        send_sem=send_sem,
+        recv_sem=recv_sem,
+        device_id=peer,
+        device_id_type=pl.DeviceIdType.MESH,
+    )
+    copy.start()
+    return copy
+
+
+def gather_kernel(in_ref, out_ref, own_sem, z_send, z_recv, send, recv):
+    z, x, core, y = place()
+    along_z, x_peer, core_peer, y_peer = peers(z, x, core, y)
+    rows = in_ref.shape[0] // PIECES
+    own = pltpu.make_async_copy(in_ref, out_ref.at[z, x, core, y], own_sem)
+    own.start()
+    greet(along_z, x_peer, core_peer, y_peer)
+    started = []
+    z_copies = []
+    for q in range(PIECES):
+        piece = pl.ds(q * rows, rows)
+        z_copies.append(
+            [
+                remote(
+                    in_ref.at[piece],
+                    out_ref.at[z, x, core, y, piece],
+                    z_send.at[q, i],
+                    z_recv.at[q, i],
+                    along_z[i],
+                )
+                for i in range(3)
+            ]
+        )
+    own.wait()
+    waiting = []
+    for q in range(PIECES):
+        for copy in z_copies[q]:
+            copy.wait_recv()
+        part = out_ref.at[:, x, core, y, pl.ds(q * rows, rows)]
+        peer = x_peer if q % 2 == 0 else y_peer
+        waiting.append(remote(part, part, send.at[q, 0], recv.at[q, 0], peer))
+    for q in range(PIECES):
+        waiting[q].wait_recv()
+        started.append(waiting[q])
+        piece = pl.ds(q * rows, rows)
+        if q % 2 == 0:
+            part, peer = out_ref.at[:, :, core, y, piece], y_peer
+        else:
+            part, peer = out_ref.at[:, x, core, :, piece], x_peer
+        waiting[q] = remote(part, part, send.at[q, 1], recv.at[q, 1], peer)
+    for q in range(PIECES):
+        waiting[q].wait_recv()
+        started.append(waiting[q])
+        part = out_ref.at[:, :, core, :, pl.ds(q * rows, rows)]
+        waiting[q] = remote(part, part, send.at[q, 2], recv.at[q, 2], core_peer)
+    for q in range(PIECES):
+        waiting[q].wait_recv()
+        started.append(waiting[q])
+    for copies in z_copies:
+        started.extend(copies)
+    for copy in started:
+        copy.wait_send()
+
+
+def gather_rows(normed):
+    rows, width = normed.shape
+    out = pl.pallas_call(
+        gather_kernel,
+        out_shape=jax.ShapeDtypeStruct((4, 2, 2, 2, rows, width), normed.dtype),
+        in_specs=[pl.BlockSpec(memory_space=pltpu.VMEM)],
+        out_specs=pl.BlockSpec(memory_space=pl.ANY),
+        scratch_shapes=[
+            pltpu.SemaphoreType.DMA,
+            pltpu.SemaphoreType.DMA((PIECES, 3)),
+            pltpu.SemaphoreType.DMA((PIECES, 3)),
+            pltpu.SemaphoreType.DMA((PIECES, 3)),
+            pltpu.SemaphoreType.DMA((PIECES, 3)),
+        ],
+        compiler_params=pltpu.CompilerParams(collective_id=0, has_side_effects=True),
+    )(normed)
+    return out.reshape(-1, width)
+
+
+def scatter_kernel(
+    in_ref, out_ref, in0, in1, in2, in3, sum1, sum2, sum3, z_send, z_recv, send, recv
+):
+    z, x, core, y = place()
+    along_z, x_peer, core_peer, y_peer = peers(z, x, core, y)
+    rows = in_ref.shape[4] // PIECES
+    f32 = jnp.float32
+    greet(along_z, x_peer, core_peer, y_peer)
+    started = []
+    waiting = []
+    for q in range(PIECES):
+        part = in_ref.at[:, :, 1 - core, :, pl.ds(q * rows, rows)]
+        waiting.append(remote(part, in0.at[q], send.at[q, 0], recv.at[q, 0], core_peer))
+    for q in range(PIECES):
+        waiting[q].wait_recv()
+        started.append(waiting[q])
+        piece = pl.ds(q * rows, rows)
+
+        def add_core(i, carry):
+            a, b, c = lax.div(i, 4), lax.rem(lax.div(i, 2), 2), lax.rem(i, 2)
+            total = in_ref[a, b, core, c, piece].astype(f32) + in0[q, a, b, c].astype(f32)
+            sum1[q, a, b, c] = total.astype(sum1.dtype)
+            return carry
+
+        lax.fori_loop(0, 16, add_core, 0)
+        if q % 2 == 0:
+            part, peer = sum1.at[q, :, 1 - x], x_peer
+        else:
+            part, peer = sum1.at[q, :, :, 1 - y], y_peer
+        waiting[q] = remote(part, in1.at[q], send.at[q, 1], recv.at[q, 1], peer)
+    for q in range(PIECES):
+        waiting[q].wait_recv()
+        started.append(waiting[q])
+
+        def add_first(i, carry):
+            a, b = lax.div(i, 2), lax.rem(i, 2)
+            mine = sum1[q, a, x, b] if q % 2 == 0 else sum1[q, a, b, y]
+            sum2[q, a, b] = (mine.astype(f32) + in1[q, a, b].astype(f32)).astype(sum2.dtype)
+            return carry
+
+        lax.fori_loop(0, 8, add_first, 0)
+        if q % 2 == 0:
+            part, peer = sum2.at[q, :, 1 - y], y_peer
+        else:
+            part, peer = sum2.at[q, :, 1 - x], x_peer
+        waiting[q] = remote(part, in2.at[q], send.at[q, 2], recv.at[q, 2], peer)
+    z_copies = []
+    for q in range(PIECES):
+        waiting[q].wait_recv()
+        started.append(waiting[q])
+        keep = y if q % 2 == 0 else x
+
+        def add_second(a, carry):
+            total = sum2[q, a, keep].astype(f32) + in2[q, a].astype(f32)
+            sum3[q, a] = total.astype(sum3.dtype)
+            return carry
+
+        lax.fori_loop(0, 4, add_second, 0)
+        z_copies.append(
+            [
+                remote(
+                    sum3.at[q, lax.rem(z + i + 1, 4)],
+                    in3.at[q, i],
+                    z_send.at[q, i],
+                    z_recv.at[q, i],
+                    along_z[i],
+                )
+                for i in range(3)
+            ]
+        )
+    for q in range(PIECES):
+        for copy in z_copies[q]:
+            copy.wait_recv()
+            started.append(copy)
+        total = sum3[q, z].astype(f32) + in3[q, 0].astype(f32)
+        total = total + (in3[q, 1].astype(f32) + in3[q, 2].astype(f32))
+        out_ref[pl.ds(q * rows, rows)] = total
+    for copy in started:
+        copy.wait_send()
+
+
+def scatter_sum(partial):
+    rows, width = partial.shape[0] // 32, partial.shape[1]
+    piece = (rows // PIECES, width)
+    kind = partial.dtype
+    return pl.pallas_call(
+        scatter_kernel,
+        out_shape=jax.ShapeDtypeStruct((rows, width), jnp.float32),
+        in_specs=[pl.BlockSpec(memory_space=pltpu.VMEM)],
+        out_specs=pl.BlockSpec(memory_space=pltpu.VMEM),
+        scratch_shapes=[
+            pltpu.VMEM((PIECES, 4, 2, 2, *piece), kind),
+            pltpu.VMEM((PIECES, 4, 2, *piece), kind),
+            pltpu.VMEM((PIECES, 4, *piece), kind),
+            pltpu.VMEM((PIECES, 3, *piece), kind),
+            pltpu.VMEM((PIECES, 4, 2, 2, *piece), kind),
+            pltpu.VMEM((PIECES, 4, 2, *piece), kind),
+            pltpu.VMEM((PIECES, 4, *piece), kind),
+            pltpu.SemaphoreType.DMA((PIECES, 3)),
+            pltpu.SemaphoreType.DMA((PIECES, 3)),
+            pltpu.SemaphoreType.DMA((PIECES, 3)),
+            pltpu.SemaphoreType.DMA((PIECES, 3)),
+        ],
+        compiler_params=pltpu.CompilerParams(
+            collective_id=1, has_side_effects=True, vmem_limit_bytes=60 * 1024 * 1024
+        ),
+    )(partial.reshape(4, 2, 2, 2, rows, width))
+
+
 def tp_sum_scatter(rows):
     count = lax.axis_size("tp")
     if count != 2:
@@ -128,15 +355,10 @@
     hidden = residual.astype(jnp.float32) + attn_out
     inv_norm = lax.rsqrt(jnp.mean(hidden * hidden, axis=-1, keepdims=True) + 1e-06)
     normed = (hidden * inv_norm * norm_gain).astype(jnp.bfloat16)
-    all_rows = lax.all_gather(normed, ("ep", "tp"), axis=0, tiled=True)
-    group_rows = lax.all_gather(normed, "tp", axis=0, tiled=True) if lax.axis_size("tp") != 2 else None
-    if group_rows is None:
-        other = lax.ppermute(normed, "tp", [(0, 1), (1, 0)])
-        first = lax.axis_index("tp") == 0
-        group_rows = jnp.concatenate(
-            [jnp.where(first, normed, other), jnp.where(first, other, normed)], axis=0
-        )
-    shared = tp_sum_scatter(shared_part(group_rows, shared_in, shared_out))
+    all_rows = gather_rows(normed)
+    group = routes.shape[0]
+    group_rows = lax.dynamic_slice_in_dim(all_rows, ep_me * group, group, 0)
+    shared = shared_part(group_rows, shared_in, shared_out)
     partial = None
     for item in range(local_experts):
         gate_val = jnp.dot(all_rows, expert_in[item, 0], preferred_element_type=jnp.float32)
@@ -145,16 +367,19 @@
         value = jnp.einsum("tf,df->td", active, expert_out[item], preferred_element_type=jnp.float32)
         value = value * my_weights[:, item : item + 1]
         partial = value if partial is None else partial + value
-    mixture = lax.psum_scatter(
-        partial.astype(jnp.bfloat16), ("ep", "tp"), scatter_dimension=0, tiled=True
-    )
-    return (hidden + shared + mixture.astype(jnp.float32)).astype(jnp.bfloat16)
+    partial = partial.astype(jnp.bfloat16)
+    own = lax.dynamic_slice_in_dim(partial, ep_me * group, group, 0).astype(jnp.float32) + shared
+    partial = lax.dynamic_update_slice_in_dim(
+        partial, own.astype(jnp.bfloat16), ep_me * group, 0
+    )
+    return (hidden + scatter_sum(partial)).astype(jnp.bfloat16)
 
 
 def shards(*args):
     routes, expert_in = args[4], args[6]
     experts = expert_in.shape[0] * lax.axis_size("ep")
-    if experts <= 4 * routes.shape[1]:
+    spans = lax.axis_size("ep") == 16 and lax.axis_size("tp") == 2
+    if spans and experts <= 4 * routes.shape[1]:
         return dense_shards(*args)
     return slotted_shards(*args)
 

time: 332 us -> 200 us (0.60)
  waiting for transfers between devices: 235 us -> 0.01 us
  Pallas kernels: 0 us -> 125 us
  between operations: 13.5 us -> 0.09 us
  starting transfers between devices: 7.06 us -> 3.07 us
    reduce_scatter x1 -> x0, waiting for transfers between devices: 149 us -> none  [dense_shards(): lax.psum_scatter(partial.astype(jnp.bfloat16), ('ep', 'tp'), scatter_dime...]
    pallas_call x0 -> x2, Pallas kernels: none -> 125 us  [the longest x1 65.6 us: scatter_sum(): pl.pallas_call(scatter_kernel, out_shape=jax.ShapeDtypeStruct((rows, widt...]
    all_gather x1 -> x0, waiting for transfers between devices: 56.1 us -> none  [dense_shards(): all_rows = lax.all_gather(normed, ('ep', 'tp'), axis=0, tiled=True)]
    ppermute x2 -> x1, waiting for transfers between devices: 18.8 us -> 0.01 us  [tp_sum_scatter(): arrived = lax.ppermute(away, 'tp', [(0, 1), (1, 0)])]
    ppermute x1 -> x0, waiting for transfers between devices: 11.4 us -> none  [dense_shards(): other = lax.ppermute(normed, 'tp', [(0, 1), (1, 0)])]
  transfers between devices with their start and end apart: 5 -> 1, of which waited for: 5 -> 0; matrix products, arithmetic and copies ran while one was open for 4% -> 0% of each run, Pallas kernels for 0% -> 0%
where the time goes in v1:
time: 200 us; the launch traced here: 199 us
  Pallas kernels  125 us (62%)
  matrix products  43.7 us (22%)
  blocking collectives  22 us (11%)
  other arithmetic  4.07 us (2%)
  starting transfers between devices  3.07 us (2%)
    pallas_call x1, Pallas kernels, scatter_sum(): pl.pallas_call(scatter_kernel, out_shape=jax.ShapeDtypeStruct((rows, widt...  65.6 us
    pallas_call x1, Pallas kernels, gather_rows(): pl.pallas_call(gather_kernel, out_shape=jax.ShapeDtypeStruct((4, 2, 2, 2,...  59.8 us
    all_gather x1, blocking collectives, dense_shards(): all_weights = lax.all_gather(dense_weights, 'ep', axis=0, tiled=True)  22 us
    dot_general x1, matrix products, dense_shards(): jnp.einsum('tf,df->td', active, expert_out[item], preferred_element_type=...  19.1 us
    dot_general x1, matrix products, dense_shards(): jnp.dot(all_rows, expert_in[item, 0], preferred_element_type=jnp.float32)  11.8 us
    dot_general x1, matrix products, shared_part(): jnp.einsum('tf,df->td', active, s_out, preferred_element_type=jnp.float32)  6 us
  transfers between devices with their start and end apart: 1, of which 0 were waited for; matrix products, arithmetic and copies ran while one was open for 0% of the time, Pallas kernels for 0%

profile of v1, /device:TPU:0, one launch (start us, length us, event | category | flops | bytes accessed | tf_op | source)
XLA Modules:
  0.0 199.3 jit_solution(4645575910853615732)
XLA Ops:
  0.0 0.0 copy-start
  0.0 0.0 copy-start.2
  0.0 0.0 copy-start.4
  0.0 0.0 copy-start.3
  0.0 3.1 %fusion.40 = f32[128,2048]{1,0:T(8,128)S(1)} fusion(bf16[128,1024]{1,0:T(8,128)(2,1)} %param.10, bf16[1024,2048]{1,0:T(8,128)(2,1)} %param.11), kind=kOutput, calls=%fused_computation.44 | convolution fusion | flops 536870912 | bytes 5505024 | tf_op jit(solution)/shard_map/dot_general | solution.py:354
  3.2 0.0 copy-start.1
  3.2 1.0 copy-done.1
  4.2 3.1 %collective-permute-start = (bf16[64,2048]{1,0:T(8,128)(2,1)S(1)}, bf16[64,2048]{1,0:T(8,128)(2,1)}, u32[]{:S(2)}, u32[]{:S(2)}) collective-permute-start(bf16[64,2048]{1,0:T(8,128)(2,1)S(1)} %dynamic-slice_convert_fusion), channel_id=1, source_target_pairs={{0,1},{1,0},{2,3},{3,2},{4,5},{5,4},{6,7},{7,6},{8,9},{9,8},{10,11... | collective-permute-start | bytes 786440 | tf_op jit(solution)/shard_map/ppermute | solution.py:327
  7.2 0.0 copy-done.2
  7.3 0.0 copy-done.4
  7.3 22.0 %all_gather.3 = f32[2048,16]{0,1:T(8,128)S(1)} all-gather(f32[128,16]{0,1:T(8,128)S(1)} %select_reduce_fusion), channel_id=1, replica_groups=mesh['ep'=16,'tp'=2] {'ep'}, dimensions={0}, use_global_device_ids=true | all-gather | bytes 139264 | tf_op jit(solution)/shard_map/all_gather | solution.py:351
  29.3 0.0 collective-permute-done
  29.3 1.4 multiply_reduce_fusion
  30.7 0.0 copy-done.3
  30.7 0.8 multiply_convert_fusion.2.in_ref
  31.6 59.8 %shard_map.100 = bf16[4,2,2,2,64,2048]{5,4,3,2,1,0:T(8,128)(2,1)} custom-call(bf16[64,2048]{1,0:T(8,128)(2,1)} %multiply_convert_fusion.2.in_ref), custom_call_target="tpu_custom_call" | custom-call | tf_op jit(solution)/shard_map/pallas_call | solution.py:194
  91.4 11.8 %fusion.7 = f32[2048,704]{0,1:T(8,128)} fusion(bf16[2048,2048]{1,0:T(8,128)(2,1)} %bitcast.30, bf16[1,2,2048,704]{2,3,1,0:T(8,128)(2,1)} %param.16), kind=kOutput, calls=%fused_computation.8 | convolution fusion | flops 5905580032 | bytes 17039360 | tf_op jit(solution)/shard_map/dot_general | solution.py:364
  103.2 3.6 %fusion.2 = f32[128,704]{0,1:T(8,128)} fusion(bf16[2,2048,704]{1,2,0:T(8,128)(2,1)} %param.18, bf16[2048,2048]{1,0:T(8,128)(2,1)} %bitcast.31, s32[]{:T(128)S(6)} %select_n.22), kind=kOutput, calls=%fused_computation.4 | convolution fusion | flops 369098752 | bytes 3768324 | tf_op jit(solution)/shard_map/dot_general | solution.py:40
  106.8 0.0 copy-done
  106.8 19.1 %multiply_convert_fusion = bf16[2048,2048]{1,0:T(8,128)(2,1)} fusion(f32[2048]{0:T(1024)S(1)} %bitcast.35, f32[2048,704]{0,1:T(8,128)} %fusion.7, bf16[2048,2048]{1,0:T(8,128)(2,1)} %bitcast.32, bf16[1,2048,704]{1,2,0:T(8,128)(2,1)S(1)} %copy-done, bf16[1,2,2048,704]{2,3,1,0:T(8,128)(2,1)} %param.16), kind=kOutput, calls=%fused_computation | convolution fusion | flops 11828199424 | bytes 28319744 | tf_op jit(solution)/shard_map/tf,df->td/dot_general | solution.py:367
  125.9 6.0 %fusion.16 = bf16[2048,2048]{1,0:T(8,128)(2,1)} fusion(bf16[2048,2048]{1,0:T(8,128)(2,1)} %multiply_convert_fusion, s32[]{:T(128)S(6)} %select_n.22, bf16[2048,704]{0,1:T(8,128)(2,1)} %param.19, bf16[2,2048,704]{1,2,0:T(8,128)(2,1)} %param.18, bf16[2048,2048]{1,0:T(8,128)(2,1)} %bitcast.33, f32[128,704]{0,1:T(8,128)} %fusion.2), kind=kOutput, calls=%fused_computation.17 | convolution fusion | flops 739524608 | bytes 7701504 | tf_op jit(solution)/shard_map/tf,df->td/dot_general | solution.py:43
  131.9 65.6 %shard_map.101 = f32[64,2048]{1,0:T(8,128)} custom-call(bf16[4,2,2,2,64,2048]{5,4,3,2,1,0:T(8,128)(2,1)} %bitcast.34), custom_call_target="tpu_custom_call" | custom-call | tf_op jit(solution)/shard_map/pallas_call | solution.py:296
  197.5 1.8 add_convert_fusion
  (6 shorter events, 0.1 us)
Async XLA Ops:
  0.0 106.8 %copy-start = (bf16[1,2048,704]{1,2,0:T(8,128)(2,1)S(1)}, bf16[1,2048,704]{1,2,0:T(8,128)(2,1)}, u32[]{:S(2)}) copy-start(bf16[1,2048,704]{1,2,0:T(8,128)(2,1)} %param.17) | copy-start | bytes 8650756
  0.0 7.2 %copy-start.2 = (f32[128,6]{0,1:T(8,128)S(1)}, f32[128,6]{0,1:T(8,128)}, u32[]{:S(2)}) copy-start(f32[128,6]{0,1:T(8,128)} %param.15) | copy-start | bytes 9220
  0.0 7.3 %copy-start.4 = (s32[128,6]{0,1:T(8,128)S(1)}, s32[128,6]{0,1:T(8,128)}, u32[]{:S(2)}) copy-start(s32[128,6]{0,1:T(8,128)} %param.14) | copy-start | bytes 9220
  0.0 30.7 %copy-start.3 = (f32[2048]{0:T(1024)S(1)}, f32[2048]{0:T(1024)}, u32[]{:S(2)}) copy-start(f32[2048]{0:T(1024)} %param.13) | copy-start | bytes 24580
  3.2 1.0 copy-start.1
  4.2 25.1 %collective-permute-start = (bf16[64,2048]{1,0:T(8,128)(2,1)S(1)}, bf16[64,2048]{1,0:T(8,128)(2,1)}, u32[]{:S(2)}, u32[]{:S(2)}) collective-permute-start(bf16[64,2048]{1,0:T(8,128)(2,1)S(1)} %dynamic-slice_convert_fusion), channel_id=1, source_target_pairs={{0,1},{1,0},{2,3},{3,2},{4,5},{5,4},{6,7},{7,6},{8,9},{9,8},{10,11... | collective-permute-start | bytes 786440 | tf_op jit(solution)/shard_map/ppermute | solution.py:327

commit v2 on v1

--- a/solution.py
+++ b/solution.py
@@ -135,13 +135,22 @@
     return copy
 
 
-def gather_kernel(in_ref, out_ref, own_sem, z_send, z_recv, send, recv):
+def gather_kernel(
+    in_ref, w_ref, out_ref, w_out, own_sem, z_send, z_recv, send, recv, w_send, w_recv
+):
     z, x, core, y = place()
     along_z, x_peer, core_peer, y_peer = peers(z, x, core, y)
+    ep = lax.axis_index("ep")
     rows = in_ref.shape[0] // PIECES
     own = pltpu.make_async_copy(in_ref, out_ref.at[z, x, core, y], own_sem)
     own.start()
-    greet(along_z, x_peer, core_peer, y_peer)
+    others = [lax.rem(ep + step, 16) for step in range(1, 16)]
+    barrier = pltpu.get_barrier_semaphore()
+    for peer in [(other, y) for other in others] + [y_peer]:
+        pl.semaphore_signal(
+            barrier, inc=1, device_id=peer, device_id_type=pl.DeviceIdType.MESH
+        )
+    pl.semaphore_wait(barrier, 16)
     started = []
     z_copies = []
     for q in range(PIECES):
@@ -158,54 +167,68 @@
                 for i in range(3)
             ]
         )
+        started.extend(z_copies[q])
+    w_copies = [
+        remote(w_ref.at[other], w_out.at[ep], w_send.at[i], w_recv.at[i], (other, y))
+        for i, other in enumerate(others)
+    ]
+    w_out[ep] = w_ref[ep]
     own.wait()
-    waiting = []
-    for q in range(PIECES):
-        for copy in z_copies[q]:
-            copy.wait_recv()
-        part = out_ref.at[:, x, core, y, pl.ds(q * rows, rows)]
-        peer = x_peer if q % 2 == 0 else y_peer
-        waiting.append(remote(part, part, send.at[q, 0], recv.at[q, 0], peer))
-    for q in range(PIECES):
-        waiting[q].wait_recv()
-        started.append(waiting[q])
-        piece = pl.ds(q * rows, rows)
-        if q % 2 == 0:
-            part, peer = out_ref.at[:, :, core, y, piece], y_peer
-        else:
-            part, peer = out_ref.at[:, x, core, :, piece], x_peer
-        waiting[q] = remote(part, part, send.at[q, 1], recv.at[q, 1], peer)
-    for q in range(PIECES):
-        waiting[q].wait_recv()
-        started.append(waiting[q])
-        part = out_ref.at[:, :, core, :, pl.ds(q * rows, rows)]
-        waiting[q] = remote(part, part, send.at[q, 2], recv.at[q, 2], core_peer)
-    for q in range(PIECES):
-        waiting[q].wait_recv()
-        started.append(waiting[q])
-    for copies in z_copies:
-        started.extend(copies)
+    waiting = [None] * PIECES
+    for turn in range(PIECES + 3):
+        for stage in range(3, -1, -1):
+            q = turn - stage
+            if q < 0 or q >= PIECES:
+                continue
+            piece = pl.ds(q * rows, rows)
+            if stage == 0:
+                for copy in z_copies[q]:
+                    copy.wait_recv()
+                part = out_ref.at[:, x, core, y, piece]
+                peer = x_peer if q % 2 == 0 else y_peer
+            else:
+                waiting[q].wait_recv()
+                started.append(waiting[q])
+                if stage == 1 and q % 2 == 0:
+                    part, peer = out_ref.at[:, :, core, y, piece], y_peer
+                elif stage == 1:
+                    part, peer = out_ref.at[:, x, core, :, piece], x_peer
+                else:
+                    part, peer = out_ref.at[:, :, core, :, piece], core_peer
+            if stage < 3:
+                waiting[q] = remote(part, part, send.at[q, stage], recv.at[q, stage], peer)
+    for copy in w_copies:
+        copy.wait_recv()
+        started.append(copy)
     for copy in started:
         copy.wait_send()
 
 
-def gather_rows(normed):
+def gather_rows(normed, weights):
     rows, width = normed.shape
-    out = pl.pallas_call(
+    out, gathered = pl.pallas_call(
         gather_kernel,
-        out_shape=jax.ShapeDtypeStruct((4, 2, 2, 2, rows, width), normed.dtype),
-        in_specs=[pl.BlockSpec(memory_space=pltpu.VMEM)],
-        out_specs=pl.BlockSpec(memory_space=pl.ANY),
+        out_shape=(
+            jax.ShapeDtypeStruct((4, 2, 2, 2, rows, width), normed.dtype),
+            jax.ShapeDtypeStruct(weights.shape, weights.dtype),
+        ),
+        in_specs=[pl.BlockSpec(memory_space=pltpu.VMEM)] * 2,
+        out_specs=(
+            pl.BlockSpec(memory_space=pl.ANY),
+            pl.BlockSpec(memory_space=pltpu.VMEM),
+        ),
         scratch_shapes=[
             pltpu.SemaphoreType.DMA,
             pltpu.SemaphoreType.DMA((PIECES, 3)),
             pltpu.SemaphoreType.DMA((PIECES, 3)),
             pltpu.SemaphoreType.DMA((PIECES, 3)),
             pltpu.SemaphoreType.DMA((PIECES, 3)),
+            pltpu.SemaphoreType.DMA((15,)),
+            pltpu.SemaphoreType.DMA((15,)),
         ],
         compiler_params=pltpu.CompilerParams(collective_id=0, has_side_effects=True),
-    )(normed)
-    return out.reshape(-1, width)
+    )(normed, weights)
+    return out.reshape(-1, width), gathered
 
 
 def scatter_kernel(
@@ -221,9 +244,8 @@
     for q in range(PIECES):
         part = in_ref.at[:, :, 1 - core, :, pl.ds(q * rows, rows)]
         waiting.append(remote(part, in0.at[q], send.at[q, 0], recv.at[q, 0], core_peer))
-    for q in range(PIECES):
-        waiting[q].wait_recv()
-        started.append(waiting[q])
+
+    def after_core(q):
         piece = pl.ds(q * rows, rows)
 
         def add_core(i, carry):
@@ -237,11 +259,9 @@
             part, peer = sum1.at[q, :, 1 - x], x_peer
         else:
             part, peer = sum1.at[q, :, :, 1 - y], y_peer
-        waiting[q] = remote(part, in1.at[q], send.at[q, 1], recv.at[q, 1], peer)
-    for q in range(PIECES):
-        waiting[q].wait_recv()
-        started.append(waiting[q])
-
+        return remote(part, in1.at[q], send.at[q, 1], recv.at[q, 1], peer)
+
+    def after_first(q):
         def add_first(i, carry):
             a, b = lax.div(i, 2), lax.rem(i, 2)
             mine = sum1[q, a, x, b] if q % 2 == 0 else sum1[q, a, b, y]
@@ -253,11 +273,9 @@
             part, peer = sum2.at[q, :, 1 - y], y_peer
         else:
             part, peer = sum2.at[q, :, 1 - x], x_peer
-        waiting[q] = remote(part, in2.at[q], send.at[q, 2], recv.at[q, 2], peer)
-    z_copies = []
-    for q in range(PIECES):
-        waiting[q].wait_recv()
-        started.append(waiting[q])
+        return remote(part, in2.at[q], send.at[q, 2], recv.at[q, 2], peer)
+
+    def after_second(q):
         keep = y if q % 2 == 0 else x
 
         def add_second(a, carry):
@@ -266,25 +284,36 @@
             return carry
 
         lax.fori_loop(0, 4, add_second, 0)
-        z_copies.append(
-            [
-                remote(
-                    sum3.at[q, lax.rem(z + i + 1, 4)],
-                    in3.at[q, i],
-                    z_send.at[q, i],
-                    z_recv.at[q, i],
-                    along_z[i],
-                )
-                for i in range(3)
-            ]
-        )
-    for q in range(PIECES):
-        for copy in z_copies[q]:
-            copy.wait_recv()
-            started.append(copy)
+        return [
+            remote(
+                sum3.at[q, lax.rem(z + i + 1, 4)],
+                in3.at[q, i],
+                z_send.at[q, i],
+                z_recv.at[q, i],
+                along_z[i],
+            )
+            for i in range(3)
+        ]
+
+    def after_z(q):
         total = sum3[q, z].astype(f32) + in3[q, 0].astype(f32)
         total = total + (in3[q, 1].astype(f32) + in3[q, 2].astype(f32))
         out_ref[pl.ds(q * rows, rows)] = total
+
+    for turn in range(PIECES + 3):
+        for stage in range(4):
+            q = turn - stage
+            if q < 0 or q >= PIECES:
+                continue
+            if stage < 3:
+                waiting[q].wait_recv()
+                started.append(waiting[q])
+                waiting[q] = (after_core, after_first, after_second)[stage](q)
+            else:
+                for copy in waiting[q]:
+                    copy.wait_recv()
+                    started.append(copy)
+                after_z(q)
     for copy in started:
         copy.wait_send()
 
@@ -348,14 +377,14 @@
     weights = route_weights(route_logits)
     chosen = routes[:, :, None] == jnp.arange(experts, dtype=jnp.int32)[None, None, :]
     dense_weights = jnp.sum(jnp.where(chosen, weights[:, :, None], 0.0), axis=1)
-    all_weights = lax.all_gather(dense_weights, "ep", axis=0, tiled=True)
-    my_weights = lax.dynamic_slice_in_dim(all_weights, ep_me * local_experts, local_experts, 1)
+    out_weights = jnp.broadcast_to(dense_weights.T[:, None, :], (experts, 8, routes.shape[0]))
 
     attn_out = tp_sum_scatter(jnp.dot(attn, o_weight, preferred_element_type=jnp.float32))
     hidden = residual.astype(jnp.float32) + attn_out
     inv_norm = lax.rsqrt(jnp.mean(hidden * hidden, axis=-1, keepdims=True) + 1e-06)
     normed = (hidden * inv_norm * norm_gain).astype(jnp.bfloat16)
-    all_rows = gather_rows(normed)
+    all_rows, all_weights = gather_rows(normed, out_weights)
+    my_weights = all_weights[:, 0, :].reshape(-1, 1)
     group = routes.shape[0]
     group_rows = lax.dynamic_slice_in_dim(all_rows, ep_me * group, group, 0)
     shared = shared_part(group_rows, shared_in, shared_out)

time: 200 us -> 212 us (1.060)
  Pallas kernels: 125 us -> 152 us
  blocking collectives: 22 us -> 0 us
  waiting for transfers between devices: 0.01 us -> 6.34 us
    pallas_call x1, Pallas kernels: 59.8 us -> 88.6 us  [gather_rows(): pl.pallas_call(gather_kernel, out_shape=(jax.ShapeDtypeStruct((4, 2, 2, 2...]
    all_gather x1 -> x0, blocking collectives: 22 us -> none  [dense_shards(): all_weights = lax.all_gather(dense_weights, 'ep', axis=0, tiled=True)]
    ppermute x1, waiting for transfers between devices: 0.01 us -> 6.34 us  [tp_sum_scatter(): arrived = lax.ppermute(away, 'tp', [(0, 1), (1, 0)])]
  transfers between devices with their start and end apart: 1 -> 1, of which waited for: 0 -> 1; matrix products, arithmetic and copies ran while one was open for 0% -> 0% of each run, Pallas kernels for 0% -> 0%
where the time goes in v2:
time: 212 us
  Pallas kernels  152 us (72%)
  matrix products  43.6 us (21%)
  waiting for transfers between devices  6.34 us (3%)
  other arithmetic  4.07 us (2%)
  starting transfers between devices  3.07 us (1%)
  local copies, waits for them, and re-layouts  2.51 us (1%)
    pallas_call x1, Pallas kernels, gather_rows(): pl.pallas_call(gather_kernel, out_shape=(jax.ShapeDtypeStruct((4, 2, 2, 2...  88.6 us
    pallas_call x1, Pallas kernels, scatter_sum(): pl.pallas_call(scatter_kernel, out_shape=jax.ShapeDtypeStruct((rows, widt...  63.9 us
    dot_general x1, matrix products, dense_shards(): jnp.einsum('tf,df->td', active, expert_out[item], preferred_element_type=...  19.1 us
    dot_general x1, matrix products, dense_shards(): jnp.dot(all_rows, expert_in[item, 0], preferred_element_type=jnp.float32)  11.8 us
    ppermute x1, waiting for transfers between devices, tp_sum_scatter(): arrived = lax.ppermute(away, 'tp', [(0, 1), (1, 0)])  6.34 us
    dot_general x1, matrix products, shared_part(): jnp.einsum('tf,df->td', active, s_out, preferred_element_type=jnp.float32)  6 us
  transfers between devices with their start and end apart: 1, of which 1 were waited for; matrix products, arithmetic and copies ran while one was open for 0% of the time, Pallas kernels for 0%

profile of v2, /device:TPU:0, one launch (start us, length us, event | category | flops | bytes accessed | tf_op | source)
XLA Modules:
  0.0 212.2 jit_solution(1183223774678456241)
XLA Ops:
  0.0 0.0 copy-start
  0.0 0.0 copy-start.2
  0.0 0.0 copy-start.4
  0.0 0.0 copy-start.3
  0.0 3.1 %fusion.40 = f32[128,2048]{1,0:T(8,128)S(1)} fusion(bf16[128,1024]{1,0:T(8,128)(2,1)} %param.10, bf16[1024,2048]{1,0:T(8,128)(2,1)} %param.11), kind=kOutput, calls=%fused_computation.43 | convolution fusion | flops 536870912 | bytes 5505024 | tf_op jit(solution)/shard_map/dot_general | solution.py:382
  3.2 0.0 copy-start.1
  3.2 1.0 copy-done.1
  4.2 3.1 %collective-permute-start = (bf16[64,2048]{1,0:T(8,128)(2,1)S(1)}, bf16[64,2048]{1,0:T(8,128)(2,1)}, u32[]{:S(2)}, u32[]{:S(2)}) collective-permute-start(bf16[64,2048]{1,0:T(8,128)(2,1)S(1)} %dynamic-slice_convert_fusion), channel_id=1, source_target_pairs={{0,1},{1,0},{2,3},{3,2},{4,5},{5,4},{6,7},{7,6},{8,9},{9,8},{10,11... | collective-permute-start | bytes 786440 | tf_op jit(solution)/shard_map/ppermute | solution.py:356
  7.2 0.0 copy-done.2
  7.3 0.0 copy-done.4
  7.3 6.3 %collective-permute-done = bf16[64,2048]{1,0:T(8,128)(2,1)} collective-permute-done((bf16[64,2048]{1,0:T(8,128)(2,1)S(1)}, bf16[64,2048]{1,0:T(8,128)(2,1)}, u32[]{:S(2)}, u32[]{:S(2)}) %collective-permute-start) | collective-permute-done | bytes 262176 | tf_op jit(solution)/shard_map/ppermute | solution.py:356
  13.7 1.4 multiply_reduce_fusion
  15.1 0.0 copy-done.3
  15.1 0.8 multiply_convert_fusion.2.in_ref
  15.9 0.6 broadcast_in_dim.16.w_ref
  16.5 88.6 %shard_map.100 = (bf16[4,2,2,2,64,2048]{5,4,3,2,1,0:T(8,128)(2,1)}, f32[16,8,128]{2,1,0:T(8,128)}) custom-call(bf16[64,2048]{1,0:T(8,128)(2,1)} %multiply_convert_fusion.2.in_ref, f32[16,8,128]{2,1,0:T(8,128)} %broadcast_in_dim.16.w_ref), custom_call_target="tpu_custom_call" | custom-call | tf_op jit(solution)/shard_map/pallas_call | solution.py:209
  105.1 0.8 slice.17
  106.0 11.8 %fusion.7 = f32[2048,704]{0,1:T(8,128)} fusion(bf16[2048,2048]{1,0:T(8,128)(2,1)} %bitcast.34, bf16[1,2,2048,704]{2,3,1,0:T(8,128)(2,1)} %param.16), kind=kOutput, calls=%fused_computation.8 | convolution fusion | flops 5905580032 | bytes 17039360 | tf_op jit(solution)/shard_map/dot_general | solution.py:393
  117.8 3.6 %fusion.2 = f32[128,704]{0,1:T(8,128)} fusion(bf16[2,2048,704]{1,2,0:T(8,128)(2,1)} %param.18, bf16[2048,2048]{1,0:T(8,128)(2,1)} %bitcast.35, s32[]{:T(128)S(6)} %select_n.18), kind=kOutput, calls=%fused_computation.4 | convolution fusion | flops 369098752 | bytes 3768324 | tf_op jit(solution)/shard_map/dot_general | solution.py:40
  121.4 0.0 copy-done
  121.4 19.1 %multiply_convert_fusion = bf16[2048,2048]{1,0:T(8,128)(2,1)} fusion(f32[2048]{0:T(1024)S(1)} %bitcast.33, f32[2048,704]{0,1:T(8,128)} %fusion.7, bf16[2048,2048]{1,0:T(8,128)(2,1)} %bitcast.36, bf16[1,2048,704]{1,2,0:T(8,128)(2,1)S(1)} %copy-done, bf16[1,2,2048,704]{2,3,1,0:T(8,128)(2,1)} %param.16), kind=kOutput, calls=%fused_computation | convolution fusion | flops 11828199424 | bytes 28319744 | tf_op jit(solution)/shard_map/tf,df->td/dot_general | solution.py:396
  140.5 6.0 %fusion.16 = bf16[2048,2048]{1,0:T(8,128)(2,1)} fusion(bf16[2048,2048]{1,0:T(8,128)(2,1)} %multiply_convert_fusion, s32[]{:T(128)S(6)} %select_n.18, bf16[2048,704]{0,1:T(8,128)(2,1)} %param.19, bf16[2,2048,704]{1,2,0:T(8,128)(2,1)} %param.18, bf16[2048,2048]{1,0:T(8,128)(2,1)} %bitcast.37, f32[128,704]{0,1:T(8,128)} %fusion.2), kind=kOutput, calls=%fused_computation.17 | convolution fusion | flops 739524608 | bytes 7701504 | tf_op jit(solution)/shard_map/tf,df->td/dot_general | solution.py:43
  146.5 63.9 %shard_map.101 = f32[64,2048]{1,0:T(8,128)} custom-call(bf16[4,2,2,2,64,2048]{5,4,3,2,1,0:T(8,128)(2,1)} %bitcast.31), custom_call_target="tpu_custom_call" | custom-call | tf_op jit(solution)/shard_map/pallas_call | solution.py:325
  210.4 1.8 add_convert_fusion
  (5 shorter events, 0.1 us)
Async XLA Ops:
  0.0 121.4 %copy-start = (bf16[1,2048,704]{1,2,0:T(8,128)(2,1)S(1)}, bf16[1,2048,704]{1,2,0:T(8,128)(2,1)}, u32[]{:S(2)}) copy-start(bf16[1,2048,704]{1,2,0:T(8,128)(2,1)} %param.17) | copy-start | bytes 8650756
  0.0 7.2 %copy-start.2 = (f32[128,6]{0,1:T(8,128)S(1)}, f32[128,6]{0,1:T(8,128)}, u32[]{:S(2)}) copy-start(f32[128,6]{0,1:T(8,128)} %param.15) | copy-start | bytes 9220
  0.0 7.3 %copy-start.4 = (s32[128,6]{0,1:T(8,128)S(1)}, s32[128,6]{0,1:T(8,128)}, u32[]{:S(2)}) copy-start(s32[128,6]{0,1:T(8,128)} %param.14) | copy-start | bytes 9220
  0.0 15.1 %copy-start.3 = (f32[2048]{0:T(1024)S(1)}, f32[2048]{0:T(1024)}, u32[]{:S(2)}) copy-start(f32[2048]{0:T(1024)} %param.13) | copy-start | bytes 24580
  3.2 1.0 copy-start.1
  4.2 9.5 %collective-permute-start = (bf16[64,2048]{1,0:T(8,128)(2,1)S(1)}, bf16[64,2048]{1,0:T(8,128)(2,1)}, u32[]{:S(2)}, u32[]{:S(2)}) collective-permute-start(bf16[64,2048]{1,0:T(8,128)(2,1)S(1)} %dynamic-slice_convert_fusion), channel_id=1, source_target_pairs={{0,1},{1,0},{2,3},{3,2},{4,5},{5,4},{6,7},{7,6},{8,9},{9,8},{10,11... | collective-permute-start | bytes 786440 | tf_op jit(solution)/shard_map/ppermute | solution.py:356

commit v3 on v2

--- a/solution.py
+++ b/solution.py
@@ -6,6 +6,7 @@
 from jax.sharding import PartitionSpec as P
 
 PIECES = 4
+GATHER_STEPS = (0, 2, 5, 8)
 
 
 def slot_places(route_rows, capacity, experts):
@@ -175,28 +176,28 @@
     w_out[ep] = w_ref[ep]
     own.wait()
     waiting = [None] * PIECES
-    for turn in range(PIECES + 3):
-        for stage in range(3, -1, -1):
-            q = turn - stage
-            if q < 0 or q >= PIECES:
-                continue
-            piece = pl.ds(q * rows, rows)
-            if stage == 0:
-                for copy in z_copies[q]:
-                    copy.wait_recv()
-                part = out_ref.at[:, x, core, y, piece]
-                peer = x_peer if q % 2 == 0 else y_peer
+    order = sorted(
+        ((stage, q) for stage in range(4) for q in range(PIECES)),
+        key=lambda item: (item[1] + GATHER_STEPS[item[0]], item[0]),
+    )
+    for stage, q in order:
+        piece = pl.ds(q * rows, rows)
+        if stage == 0:
+            for copy in z_copies[q]:
+                copy.wait_recv()
+            part = out_ref.at[:, x, core, y, piece]
+            peer = x_peer if q % 2 == 0 else y_peer
+        else:
+            waiting[q].wait_recv()
+            started.append(waiting[q])
+            if stage == 1 and q % 2 == 0:
+                part, peer = out_ref.at[:, :, core, y, piece], y_peer
+            elif stage == 1:
+                part, peer = out_ref.at[:, x, core, :, piece], x_peer
             else:
-                waiting[q].wait_recv()
-                started.append(waiting[q])
-                if stage == 1 and q % 2 == 0:
-                    part, peer = out_ref.at[:, :, core, y, piece], y_peer
-                elif stage == 1:
-                    part, peer = out_ref.at[:, x, core, :, piece], x_peer
-                else:
-                    part, peer = out_ref.at[:, :, core, :, piece], core_peer
-            if stage < 3:
-                waiting[q] = remote(part, part, send.at[q, stage], recv.at[q, stage], peer)
+                part, peer = out_ref.at[:, :, core, :, piece], core_peer
+        if stage < 3:
+            waiting[q] = remote(part, part, send.at[q, stage], recv.at[q, stage], peer)
     for copy in w_copies:
         copy.wait_recv()
         started.append(copy)

time: 212 us -> 185 us (0.87)
  Pallas kernels: 152 us -> 125 us
    pallas_call x1, Pallas kernels: 88.6 us -> 62.6 us  [gather_rows(): pl.pallas_call(gather_kernel, out_shape=(jax.ShapeDtypeStruct((4, 2, 2, 2...]
where the time goes in v3:
time: 185 us
  Pallas kernels  125 us (68%)
  matrix products  43.6 us (24%)
  waiting for transfers between devices  6.34 us (3%)
  other arithmetic  4.07 us (2%)
  starting transfers between devices  3.07 us (2%)
  local copies, waits for them, and re-layouts  2.51 us (1%)
    pallas_call x1, Pallas kernels, scatter_sum(): pl.pallas_call(scatter_kernel, out_shape=jax.ShapeDtypeStruct((rows, widt...  62.6 us
    pallas_call x1, Pallas kernels, gather_rows(): pl.pallas_call(gather_kernel, out_shape=(jax.ShapeDtypeStruct((4, 2, 2, 2...  62.6 us
    dot_general x1, matrix products, dense_shards(): jnp.einsum('tf,df->td', active, expert_out[item], preferred_element_type=...  19.1 us
    dot_general x1, matrix products, dense_shards(): jnp.dot(all_rows, expert_in[item, 0], preferred_element_type=jnp.float32)  11.8 us
    ppermute x1, waiting for transfers between devices, tp_sum_scatter(): arrived = lax.ppermute(away, 'tp', [(0, 1), (1, 0)])  6.34 us
    dot_general x1, matrix products, shared_part(): jnp.einsum('tf,df->td', active, s_out, preferred_element_type=jnp.float32)  6 us
  transfers between devices with their start and end apart: 1, of which 1 were waited for; matrix products, arithmetic and copies ran while one was open for 0% of the time, Pallas kernels for 0%

profile of v3, /device:TPU:0, one launch (start us, length us, event | category | flops | bytes accessed | tf_op | source)
XLA Modules:
  0.0 184.9 jit_solution(4458575927542361870)
XLA Ops:
  0.0 0.0 copy-start
  0.0 0.0 copy-start.2
  0.0 0.0 copy-start.4
  0.0 0.0 copy-start.3
  0.0 3.1 %fusion.40 = f32[128,2048]{1,0:T(8,128)S(1)} fusion(bf16[128,1024]{1,0:T(8,128)(2,1)} %param.10, bf16[1024,2048]{1,0:T(8,128)(2,1)} %param.11), kind=kOutput, calls=%fused_computation.43 | convolution fusion | flops 536870912 | bytes 5505024 | tf_op jit(solution)/shard_map/dot_general | solution.py:383
  3.2 0.0 copy-start.1
  3.2 1.0 copy-done.1
  4.2 3.1 %collective-permute-start = (bf16[64,2048]{1,0:T(8,128)(2,1)S(1)}, bf16[64,2048]{1,0:T(8,128)(2,1)}, u32[]{:S(2)}, u32[]{:S(2)}) collective-permute-start(bf16[64,2048]{1,0:T(8,128)(2,1)S(1)} %dynamic-slice_convert_fusion), channel_id=1, source_target_pairs={{0,1},{1,0},{2,3},{3,2},{4,5},{5,4},{6,7},{7,6},{8,9},{9,8},{10,11... | collective-permute-start | bytes 786440 | tf_op jit(solution)/shard_map/ppermute | solution.py:357
  7.2 0.0 copy-done.2
  7.3 0.0 copy-done.4
  7.3 6.3 %collective-permute-done = bf16[64,2048]{1,0:T(8,128)(2,1)} collective-permute-done((bf16[64,2048]{1,0:T(8,128)(2,1)S(1)}, bf16[64,2048]{1,0:T(8,128)(2,1)}, u32[]{:S(2)}, u32[]{:S(2)}) %collective-permute-start) | collective-permute-done | bytes 262176 | tf_op jit(solution)/shard_map/ppermute | solution.py:357
  13.7 1.4 multiply_reduce_fusion
  15.1 0.0 copy-done.3
  15.1 0.8 multiply_convert_fusion.2.in_ref
  15.9 0.6 broadcast_in_dim.16.w_ref
  16.5 62.6 %shard_map.100 = (bf16[4,2,2,2,64,2048]{5,4,3,2,1,0:T(8,128)(2,1)}, f32[16,8,128]{2,1,0:T(8,128)}) custom-call(bf16[64,2048]{1,0:T(8,128)(2,1)} %multiply_convert_fusion.2.in_ref, f32[16,8,128]{2,1,0:T(8,128)} %broadcast_in_dim.16.w_ref), custom_call_target="tpu_custom_call" | custom-call | tf_op jit(solution)/shard_map/pallas_call | solution.py:210
  79.1 0.8 slice.17
  80.0 11.8 %fusion.7 = f32[2048,704]{0,1:T(8,128)} fusion(bf16[2048,2048]{1,0:T(8,128)(2,1)} %bitcast.34, bf16[1,2,2048,704]{2,3,1,0:T(8,128)(2,1)} %param.16), kind=kOutput, calls=%fused_computation.8 | convolution fusion | flops 5905580032 | bytes 17039360 | tf_op jit(solution)/shard_map/dot_general | solution.py:394
  91.8 3.6 %fusion.2 = f32[128,704]{0,1:T(8,128)} fusion(bf16[2,2048,704]{1,2,0:T(8,128)(2,1)} %param.18, bf16[2048,2048]{1,0:T(8,128)(2,1)} %bitcast.35, s32[]{:T(128)S(6)} %select_n.18), kind=kOutput, calls=%fused_computation.4 | convolution fusion | flops 369098752 | bytes 3768324 | tf_op jit(solution)/shard_map/dot_general | solution.py:41
  95.4 0.0 copy-done
  95.4 19.1 %multiply_convert_fusion = bf16[2048,2048]{1,0:T(8,128)(2,1)} fusion(f32[2048]{0:T(1024)S(1)} %bitcast.33, f32[2048,704]{0,1:T(8,128)} %fusion.7, bf16[2048,2048]{1,0:T(8,128)(2,1)} %bitcast.36, bf16[1,2048,704]{1,2,0:T(8,128)(2,1)S(1)} %copy-done, bf16[1,2,2048,704]{2,3,1,0:T(8,128)(2,1)} %param.16), kind=kOutput, calls=%fused_computation | convolution fusion | flops 11828199424 | bytes 28319744 | tf_op jit(solution)/shard_map/tf,df->td/dot_general | solution.py:397
  114.5 6.0 %fusion.16 = bf16[2048,2048]{1,0:T(8,128)(2,1)} fusion(bf16[2048,2048]{1,0:T(8,128)(2,1)} %multiply_convert_fusion, s32[]{:T(128)S(6)} %select_n.18, bf16[2048,704]{0,1:T(8,128)(2,1)} %param.19, bf16[2,2048,704]{1,2,0:T(8,128)(2,1)} %param.18, bf16[2048,2048]{1,0:T(8,128)(2,1)} %bitcast.37, f32[128,704]{0,1:T(8,128)} %fusion.2), kind=kOutput, calls=%fused_computation.17 | convolution fusion | flops 739524608 | bytes 7701504 | tf_op jit(solution)/shard_map/tf,df->td/dot_general | solution.py:44
  120.5 62.6 %shard_map.101 = f32[64,2048]{1,0:T(8,128)} custom-call(bf16[4,2,2,2,64,2048]{5,4,3,2,1,0:T(8,128)(2,1)} %bitcast.31), custom_call_target="tpu_custom_call" | custom-call | tf_op jit(solution)/shard_map/pallas_call | solution.py:326
  183.1 1.8 add_convert_fusion
  (5 shorter events, 0.1 us)
Async XLA Ops:
  0.0 95.4 %copy-start = (bf16[1,2048,704]{1,2,0:T(8,128)(2,1)S(1)}, bf16[1,2048,704]{1,2,0:T(8,128)(2,1)}, u32[]{:S(2)}) copy-start(bf16[1,2048,704]{1,2,0:T(8,128)(2,1)} %param.17) | copy-start | bytes 8650756
  0.0 7.2 %copy-start.2 = (f32[128,6]{0,1:T(8,128)S(1)}, f32[128,6]{0,1:T(8,128)}, u32[]{:S(2)}) copy-start(f32[128,6]{0,1:T(8,128)} %param.15) | copy-start | bytes 9220
  0.0 7.3 %copy-start.4 = (s32[128,6]{0,1:T(8,128)S(1)}, s32[128,6]{0,1:T(8,128)}, u32[]{:S(2)}) copy-start(s32[128,6]{0,1:T(8,128)} %param.14) | copy-start | bytes 9220
  0.0 15.1 %copy-start.3 = (f32[2048]{0:T(1024)S(1)}, f32[2048]{0:T(1024)}, u32[]{:S(2)}) copy-start(f32[2048]{0:T(1024)} %param.13) | copy-start | bytes 24580
  3.2 1.0 copy-start.1
  4.2 9.5 %collective-permute-start = (bf16[64,2048]{1,0:T(8,128)(2,1)S(1)}, bf16[64,2048]{1,0:T(8,128)(2,1)}, u32[]{:S(2)}, u32[]{:S(2)}) collective-permute-start(bf16[64,2048]{1,0:T(8,128)(2,1)S(1)} %dynamic-slice_convert_fusion), channel_id=1, source_target_pairs={{0,1},{1,0},{2,3},{3,2},{4,5},{5,4},{6,7},{7,6},{8,9},{9,8},{10,11... | collective-permute-start | bytes 786440 | tf_op jit(solution)/shard_map/ppermute | solution.py:357
